TPU v7x, 32 devices: a whole 2x2x4 slice. The times are simulated.
32 devices in a mesh: blk: 4 (over z), grp: 8 (over y, x, core).
Axes of the slice: x: 2, y: 2, z: 4, core: 2. Of those that a mesh axis runs over, the one named last changes fastest.
Arguments:
- basis: bfloat16 [8, 512, 1152], P('grp', 'blk'), may hold values from -6 to 6
- coeffs: bfloat16 [2, 1152, 768], replicated, may hold values from -0.1875 to 0.1875
- stiff_blocks: bfloat16 [8, 4, 4, 128, 128], P('grp', 'blk'), as said below
- mass_blocks: bfloat16 [8, 4, 4, 128, 128], P('grp', 'blk'), as said below
- block_cols: int32 [8, 4, 4], P('grp', 'blk'), may hold values from 0 to 3
Outputs:
- basis_out: bfloat16 [8, 512, 1152], P('grp', 'blk')
- ritz_value: float32 [384], replicated
- gram: float32 [1152, 2, 1152], P('grp', None, 'blk')
Inputs may be any that keep to these rules, and one draw needn't show every extreme that they name: block_cols names row blocks of the same substructure. `mass_blocks`: real-valued blocks of order 1 / sqrt(512). `stiff_blocks`: real-valued blocks, of larger size than the mass blocks.
All inputs are finite; a program needn't handle non-finite values.
Results may differ from a plain program's by a relative error of at most 0.02.
Values may be sent and summed in bfloat16 or wider, within the bound.
No kernel may reach another device: no remote copies, remote signals or barrier semaphores. Data moves between devices by JAX's collectives and lax.ppermute only.
A program may use at most 64 MiB of HBM per device.

v0:
```python
import jax
import jax.numpy as jnp
from jax import lax
from jax.sharding import PartitionSpec as P

epsilon = 1e-06


def apply_pair(stiff, mass, cols, field, final):
    columns = field.shape[1]
    block_rows, slots = cols.shape
    edge = stiff.shape[-1]
    own_blocks = field.reshape(block_rows, edge, columns)
    wanted = cols.reshape(-1)

    def take_blocks(arrived):
        arrived_count = arrived.shape[0]
        ident = jnp.arange(arrived_count, dtype=jnp.int32)
        selector = (wanted[:, None] == ident[None, :]).astype(jnp.bfloat16)
        taken = jnp.dot(
            selector, arrived.reshape(arrived_count, -1), preferred_element_type=jnp.float32
        )
        return taken.astype(jnp.bfloat16)

    if final:
        gathered = take_blocks(lax.all_gather(own_blocks, "blk", axis=0, tiled=True))
    else:
        gathered = take_blocks(lax.all_gather(own_blocks, "blk", axis=0, tiled=True))
    gathered = gathered.reshape(block_rows, slots, edge, columns)
    contract = (((1, 3), (1, 2)), ((0,), (0,)))
    stiff_out = lax.dot_general(stiff, gathered, contract, preferred_element_type=jnp.float32)
    mass_out = lax.dot_general(mass, gathered, contract, preferred_element_type=jnp.float32)
    return (
        stiff_out.reshape(block_rows * edge, columns),
        mass_out.reshape(block_rows * edge, columns),
    )


def body(basis, coeffs, stiff_blocks, mass_blocks, block_cols):
    stiff = stiff_blocks[0]
    mass = mass_blocks[0]
    cols = block_cols[0]
    current = basis[0]
    rows_here, columns = current.shape
    mode_count = columns // 3
    total_rows = rows_here * lax.axis_size("blk") * lax.axis_size("grp")
    for sweep in range(coeffs.shape[0]):
        turned = jnp.dot(current, coeffs[sweep], preferred_element_type=jnp.float32).astype(
            jnp.bfloat16
        )
        next_modes = turned[:, :mode_count]
        next_history = turned[:, mode_count:]
        stiff_x, mass_x = apply_pair(stiff, mass, cols, next_modes, False)
        numerator, denominator = lax.psum(
            (jnp.sum(stiff_x * mass_x, axis=0), jnp.sum(mass_x * mass_x, axis=0)), ("blk", "grp")
        )
        ritz_value = numerator / (denominator + epsilon)
        residual = stiff_x - ritz_value * mass_x
        resid_sum = lax.psum(jnp.sum(residual * residual, axis=0), ("blk", "grp"))
        next_search = (residual * lax.rsqrt(resid_sum / total_rows + epsilon)).astype(jnp.bfloat16)
        current = jnp.concatenate([next_modes, next_search, next_history], axis=1)
    stiff_rest, mass_rest = apply_pair(stiff, mass, cols, current[:, mode_count:], True)
    stiff_all = jnp.concatenate(
        [stiff_x.astype(jnp.bfloat16), stiff_rest.astype(jnp.bfloat16)], axis=1
    )
    mass_all = jnp.concatenate(
        [mass_x.astype(jnp.bfloat16), mass_rest.astype(jnp.bfloat16)], axis=1
    )
    inner = (((0,), (0,)), ((), ()))
    gram_stiff = lax.dot_general(current, stiff_all, inner, preferred_element_type=jnp.float32)
    gram_mass = lax.dot_general(current, mass_all, inner, preferred_element_type=jnp.float32)
    by_group = lax.psum_scatter(
        jnp.stack([gram_stiff, gram_mass], axis=1).astype(jnp.bfloat16),
        "grp",
        scatter_dimension=0,
        tiled=True,
    )
    gram = lax.psum_scatter(by_group, "blk", scatter_dimension=2, tiled=True).astype(jnp.float32)
    return (current[None], ritz_value, gram)


def solution(mesh):
    in_specs = (
        P("grp", "blk", None),
        P(),
        P("grp", "blk", None, None, None),
        P("grp", "blk", None, None, None),
        P("grp", "blk", None),
    )
    out_specs = (P("grp", "blk", None), P(), P("grp", None, "blk"))
    return jax.shard_map(body, mesh=mesh, in_specs=in_specs, out_specs=out_specs, check_vma=False)
```

profile of v0, /device:TPU:0, one launch (start us, length us, event | category | flops | bytes accessed | tf_op | source)
XLA Modules:
  0.0 328.8 jit_solution(17541428477707894250)
XLA Ops:
  7.3 0.9 copy-done
  8.1 1.9 fusion.8
  10.1 16.2 %all-gather = bf16[512,384]{1,0:T(8,128)(2,1)S(1)} all-gather(bf16[128,384]{1,0:T(8,128)(2,1)S(1)} %get-tuple-element.22), channel_id=2, replica_groups=mesh['blk'=4,'grp'=8] {'blk'}, dimensions={0}, use_global_device_ids=true | all-gather | bytes 491520 | tf_op jit(solution)/shard_map/all_gather | solution.py:28
  27.4 40.9 %all-reduce.1 = (f32[384]{0:T(512)S(1)}, f32[384]{0:T(512)S(1)}) all-reduce(f32[384]{0:T(512)S(1)} %get-tuple-element.12, f32[384]{0:T(512)S(1)} %get-tuple-element.11), channel_id=1, replica_groups=mesh['blk'=4,'grp'=8] {'blk','grp'}, use_global_device_ids=true, to_apply=%region_1.0 | all-reduce | flops 768 | bytes 6144 | tf_op jit(solution)/shard_map/psum | solution.py:54
  68.3 40.3 %psum.44 = f32[384]{0:T(512)S(1)} all-reduce(f32[384]{0:T(512)S(1)} %multiply_reduce_fusion.3), channel_id=1, replica_groups=mesh['blk'=4,'grp'=8] {'blk','grp'}, use_global_device_ids=true, to_apply=%region_5.0 | all-reduce | flops 384 | bytes 3072 | tf_op jit(solution)/shard_map/psum | solution.py:59
  108.7 1.9 fusion.11
  110.6 14.9 %all-gather.1 = bf16[512,384]{1,0:T(8,128)(2,1)S(1)} all-gather(bf16[128,384]{1,0:T(8,128)(2,1)S(1)} %get-tuple-element.20), channel_id=3, replica_groups=mesh['blk'=4,'grp'=8] {'blk'}, dimensions={0}, use_global_device_ids=true | all-gather | bytes 491520 | tf_op jit(solution)/shard_map/all_gather | solution.py:28
  126.6 39.9 %all-reduce = (f32[384]{0:T(512)S(1)}, f32[384]{0:T(512)S(1)}) all-reduce(f32[384]{0:T(512)S(1)} %get-tuple-element.10, f32[384]{0:T(512)S(1)} %get-tuple-element.9), channel_id=1, replica_groups=mesh['blk'=4,'grp'=8] {'blk','grp'}, use_global_device_ids=true, to_apply=%region_7.0 | all-reduce | flops 768 | bytes 6144 | tf_op jit(solution)/shard_map/psum | solution.py:54
  166.5 40.4 %psum.47 = f32[384]{0:T(512)S(1)} all-reduce(f32[384]{0:T(512)S(1)} %multiply_reduce_fusion), channel_id=1, replica_groups=mesh['blk'=4,'grp'=8] {'blk','grp'}, use_global_device_ids=true, to_apply=%region_11.0 | all-reduce | flops 384 | bytes 3072 | tf_op jit(solution)/shard_map/psum | solution.py:59
  207.0 18.3 %all-gather.2 = bf16[512,768]{1,0:T(8,128)(2,1)S(1)} all-gather(bf16[128,768]{1,0:T(8,128)(2,1)S(1)} %pad_maximum_fusion.2), channel_id=4, replica_groups=mesh['blk'=4,'grp'=8] {'blk'}, dimensions={0}, use_global_device_ids=true | all-gather | bytes 983040 | tf_op jit(solution)/shard_map/all_gather | solution.py:26
  225.3 0.6 reshape.93
  225.9 0.6 convolution_convert_fusion
  226.5 0.4 fusion.16
  226.9 0.4 fusion.17
  227.6 0.9 fusion
  228.5 0.9 fusion.1
  229.4 2.8 pad_maximum_fusion
  232.3 57.6 %reduce-scatter.5.cloned.1.call-done = bf16[144,2,1152]{2,0,1:T(8,128)(2,1)} async-done(((bf16[1152,2,1152]{2,0,1:T(8,128)(2,1)}), bf16[144,2,1152]{2,0,1:T(8,128)(2,1)}) %reduce-scatter.5.cloned.1.call-update) | async-done | bytes 663568 | tf_op jit(solution)/shard_map/reduce_scatter | solution.py:72
  289.9 3.5 %copy.28 = bf16[144,2,1152]{0,1,2:T(2,128)(2,1)S(1)} copy(bf16[144,2,1152]{2,0,1:T(8,128)(2,1)} %reduce-scatter.5.cloned.1.call-done) | data formatting | bytes 1327104
  293.4 1.5 reshape.107
  295.0 0.7 fusion.54
  295.7 24.0 %reduce-scatter.7.cloned.1.call-done = bf16[288,288]{1,0:T(8,128)(2,1)} async-done(((bf16[1152,288]{1,0:T(8,128)(2,1)}), bf16[288,288]{1,0:T(8,128)(2,1)}) %reduce-scatter.7.cloned.1.call-update) | async-done | bytes 165904
  319.7 1.1 reshape.108
  321.0 0.9 copy.21
  (35 shorter events, 3.0 us)
Async XLA Ops:
  7.2 1.0 copy-start
  7.2 19.3 %copy-start.4 = (s32[1,1,4]{2,1,0:T(1,128)S(1)}, s32[1,1,4]{2,1,0:T(1,128)}, u32[]{:S(2)}) copy-start(s32[1,1,4]{2,1,0:T(1,128)} %param.9) | copy-start | bytes 52
  7.2 19.7 %copy-start.2 = (bf16[1,1,4,128,128]{4,3,2,1,0:T(8,128)(2,1)S(1)}, bf16[1,1,4,128,128]{4,3,2,1,0:T(8,128)(2,1)}, u32[]{:S(2)}) copy-start(bf16[1,1,4,128,128]{4,3,2,1,0:T(8,128)(2,1)} %param.7) | copy-start | bytes 393220
  7.2 19.9 %copy-start.1 = (bf16[1,1,4,128,128]{4,3,2,1,0:T(8,128)(2,1)S(1)}, bf16[1,1,4,128,128]{4,3,2,1,0:T(8,128)(2,1)}, u32[]{:S(2)}) copy-start(bf16[1,1,4,128,128]{4,3,2,1,0:T(8,128)(2,1)} %param.8) | copy-start | bytes 393220
  7.2 282.7 %reduce-scatter.5.cloned.1.call-start = ((), (), s32[]{:S(2)}) async-start(), calls=%async_computation.2 | async-start | bytes 5971968 | tf_op jit(solution)/shard_map/reduce_scatter | solution.py:72
  166.5 60.0 %copy-start.3 = (f32[384]{0:T(512)}, f32[384]{0:T(512)S(1)}, u32[]{:S(2)}) copy-start(f32[384]{0:T(512)S(1)} %add_divide_fusion) | copy-start | bytes 4612
  232.3 87.4 %reduce-scatter.7.cloned.1.call-start = ((), (), s32[]{:S(2)}) async-start(), calls=%async_computation.3 | async-start | bytes 1105920
Sparse Core Ops, SparseCore 0:
  232.4 57.4 reduce-scatter.4
  295.1 24.5 reduce-scatter.6
where the time goes:
time: 330 us; the launch traced here: 329 us
  blocking collectives  211 us (64%)
  waiting for transfers between devices  81.6 us (25%)
  between operations  14.3 us (4%)
  local copies, waits for them, and re-layouts  9.36 us (3%)
  matrix products  8.84 us (3%)
  other arithmetic  3.82 us (1%)
    psum x2, blocking collectives, body(): lax.psum((jnp.sum(stiff_x * mass_x, axis=0), jnp.sum(mass_x * mass_x, axi...  80.8 us
    psum x2, blocking collectives, body(): resid_sum = lax.psum(jnp.sum(residual * residual, axis=0), ('blk', 'grp'))  80.7 us
    reduce_scatter x1, waiting for transfers between devices, body(): lax.psum_scatter(jnp.stack([gram_stiff, gram_mass], axis=1).astype(jnp.bf...  57.6 us
    all_gather x3, blocking collectives, apply_pair(): lax.all_gather(own_blocks, 'blk', axis=0, tiled=True)  49.4 us
    unnamed x3, waiting for transfers between devices  24 us
    unnamed x15, local copies, waits for them, and re-layouts  8.2 us
  transfers between devices with their start and end apart: 2, of which 2 were waited for; matrix products, arithmetic and copies ran while one was open for 0% of the time, Pallas kernels for 0%

commit v1 on v0

--- a/solution.py
+++ b/solution.py
@@ -56,7 +56,9 @@
         )
         ritz_value = numerator / (denominator + epsilon)
         residual = stiff_x - ritz_value * mass_x
-        resid_sum = lax.psum(jnp.sum(residual * residual, axis=0), ("blk", "grp"))
+        resid_sum = jnp.sum(
+            lax.all_gather(jnp.sum(residual * residual, axis=0), ("blk", "grp")), axis=0
+        )
         next_search = (residual * lax.rsqrt(resid_sum / total_rows + epsilon)).astype(jnp.bfloat16)
         current = jnp.concatenate([next_modes, next_search, next_history], axis=1)
     stiff_rest, mass_rest = apply_pair(stiff, mass, cols, current[:, mode_count:], True)

time: 330 us -> 324 us (0.982)
  blocking collectives: 211 us -> 207 us
    psum x2 -> x0, blocking collectives: 80.7 us -> none  [body(): resid_sum = lax.psum(jnp.sum(residual * residual, axis=0), ('blk', 'grp'))]
    all_gather x0 -> x2, blocking collectives: none -> 79.7 us  [body(): lax.all_gather(jnp.sum(residual * residual, axis=0), ('blk', 'grp'))]
    unnamed x15 -> x17, local copies, waits for them, and re-layouts: 8.2 us -> 8.22 us
where the time goes in v1:
time: 324 us; the launch traced here: 323 us
  blocking collectives  207 us (64%)
  waiting for transfers between devices  79.1 us (24%)
  between operations  14.3 us (4%)
  local copies, waits for them, and re-layouts  9.37 us (3%)
  matrix products  8.85 us (3%)
  other arithmetic  3.95 us (1%)
    all_gather x2, blocking collectives, body(): lax.all_gather(jnp.sum(residual * residual, axis=0), ('blk', 'grp'))  79.7 us
    psum x2, blocking collectives, body(): lax.psum((jnp.sum(stiff_x * mass_x, axis=0), jnp.sum(mass_x * mass_x, axi...  78.5 us
    reduce_scatter x1, waiting for transfers between devices, body(): lax.psum_scatter(jnp.stack([gram_stiff, gram_mass], axis=1).astype(jnp.bf...  55.1 us
    all_gather x3, blocking collectives, apply_pair(): lax.all_gather(own_blocks, 'blk', axis=0, tiled=True)  49.2 us
    unnamed x3, waiting for transfers between devices  24 us
    unnamed x17, local copies, waits for them, and re-layouts  8.22 us
  transfers between devices with their start and end apart: 2, of which 2 were waited for; matrix products, arithmetic and copies ran while one was open for 0% of the time, Pallas kernels for 0%

profile of v1, /device:TPU:0, one launch (start us, length us, event | category | flops | bytes accessed | tf_op | source)
XLA Modules:
  0.0 323.0 jit_solution(13962702581953938422)
XLA Ops:
  7.3 0.9 copy-done
  8.1 1.9 fusion.8
  10.1 16.2 %all-gather = bf16[512,384]{1,0:T(8,128)(2,1)S(1)} all-gather(bf16[128,384]{1,0:T(8,128)(2,1)S(1)} %get-tuple-element.22), channel_id=2, replica_groups=mesh['blk'=4,'grp'=8] {'blk'}, dimensions={0}, use_global_device_ids=true | all-gather | bytes 491520 | tf_op jit(solution)/shard_map/all_gather | solution.py:28
  27.4 40.9 %all-reduce.1 = (f32[384]{0:T(512)S(1)}, f32[384]{0:T(512)S(1)}) all-reduce(f32[384]{0:T(512)S(1)} %get-tuple-element.12, f32[384]{0:T(512)S(1)} %get-tuple-element.11), channel_id=1, replica_groups=mesh['blk'=4,'grp'=8] {'blk','grp'}, use_global_device_ids=true, to_apply=%region_1.0 | all-reduce | flops 768 | bytes 6144 | tf_op jit(solution)/shard_map/psum | solution.py:54
  68.4 39.7 %all-gather.5 = f32[32,1,384]{2,1,0:T(1,128)S(1)} all-gather(f32[1,1,384]{2,1,0:T(1,128)S(1)} %reshape.111), channel_id=3, replica_groups=mesh['blk'=4,'grp'=8] {'blk','grp'}, dimensions={0}, use_global_device_ids=true | all-gather | bytes 50688 | tf_op jit(solution)/shard_map/all_gather | solution.py:60
  108.1 1.9 fusion.11
  110.1 15.2 %all-gather.2 = bf16[512,384]{1,0:T(8,128)(2,1)S(1)} all-gather(bf16[128,384]{1,0:T(8,128)(2,1)S(1)} %get-tuple-element.20), channel_id=4, replica_groups=mesh['blk'=4,'grp'=8] {'blk'}, dimensions={0}, use_global_device_ids=true | all-gather | bytes 491520 | tf_op jit(solution)/shard_map/all_gather | solution.py:28
  126.3 37.6 %all-reduce = (f32[384]{0:T(512)S(1)}, f32[384]{0:T(512)S(1)}) all-reduce(f32[384]{0:T(512)S(1)} %get-tuple-element.10, f32[384]{0:T(512)S(1)} %get-tuple-element.9), channel_id=1, replica_groups=mesh['blk'=4,'grp'=8] {'blk','grp'}, use_global_device_ids=true, to_apply=%region_7.0 | all-reduce | flops 768 | bytes 6144 | tf_op jit(solution)/shard_map/psum | solution.py:54
  164.0 40.0 %all-gather.6 = f32[32,1,384]{2,1,0:T(1,128)S(1)} all-gather(f32[1,1,384]{2,1,0:T(1,128)S(1)} %reshape.113), channel_id=5, replica_groups=mesh['blk'=4,'grp'=8] {'blk','grp'}, dimensions={0}, use_global_device_ids=true | all-gather | bytes 50688 | tf_op jit(solution)/shard_map/all_gather | solution.py:60
  204.2 17.7 %all-gather.4 = bf16[512,768]{1,0:T(8,128)(2,1)S(1)} all-gather(bf16[128,768]{1,0:T(8,128)(2,1)S(1)} %pad_maximum_fusion.2), channel_id=6, replica_groups=mesh['blk'=4,'grp'=8] {'blk'}, dimensions={0}, use_global_device_ids=true | all-gather | bytes 983040 | tf_op jit(solution)/shard_map/all_gather | solution.py:26
  222.0 0.6 reshape.101
  222.5 0.6 convolution_convert_fusion
  223.2 0.4 fusion.16
  223.6 0.4 fusion.17
  224.3 0.9 fusion
  225.2 0.9 fusion.1
  226.1 2.8 pad_maximum_fusion
  229.0 55.1 %reduce-scatter.5.cloned.1.call-done = bf16[144,2,1152]{2,0,1:T(8,128)(2,1)} async-done(((bf16[1152,2,1152]{2,0,1:T(8,128)(2,1)}), bf16[144,2,1152]{2,0,1:T(8,128)(2,1)}) %reduce-scatter.5.cloned.1.call-update) | async-done | bytes 663568 | tf_op jit(solution)/shard_map/reduce_scatter | solution.py:74
  284.1 3.5 %copy.28 = bf16[144,2,1152]{0,1,2:T(2,128)(2,1)S(1)} copy(bf16[144,2,1152]{2,0,1:T(8,128)(2,1)} %reduce-scatter.5.cloned.1.call-done) | data formatting | bytes 1327104
  287.6 1.5 reshape.123
  289.2 0.7 fusion.54
  289.9 24.0 %reduce-scatter.7.cloned.1.call-done = bf16[288,288]{1,0:T(8,128)(2,1)} async-done(((bf16[1152,288]{1,0:T(8,128)(2,1)}), bf16[288,288]{1,0:T(8,128)(2,1)}) %reduce-scatter.7.cloned.1.call-update) | async-done | bytes 165904
  313.9 1.1 reshape.124
  315.3 0.9 copy.21
  (39 shorter events, 3.1 us)
Async XLA Ops:
  7.2 1.0 copy-start
  7.2 19.3 %copy-start.4 = (s32[1,1,4]{2,1,0:T(1,128)S(1)}, s32[1,1,4]{2,1,0:T(1,128)}, u32[]{:S(2)}) copy-start(s32[1,1,4]{2,1,0:T(1,128)} %param.9) | copy-start | bytes 52
  7.2 19.7 %copy-start.2 = (bf16[1,1,4,128,128]{4,3,2,1,0:T(8,128)(2,1)S(1)}, bf16[1,1,4,128,128]{4,3,2,1,0:T(8,128)(2,1)}, u32[]{:S(2)}) copy-start(bf16[1,1,4,128,128]{4,3,2,1,0:T(8,128)(2,1)} %param.7) | copy-start | bytes 393220
  7.2 19.9 %copy-start.1 = (bf16[1,1,4,128,128]{4,3,2,1,0:T(8,128)(2,1)S(1)}, bf16[1,1,4,128,128]{4,3,2,1,0:T(8,128)(2,1)}, u32[]{:S(2)}) copy-start(bf16[1,1,4,128,128]{4,3,2,1,0:T(8,128)(2,1)} %param.8) | copy-start | bytes 393220
  7.2 276.9 %reduce-scatter.5.cloned.1.call-start = ((), (), s32[]{:S(2)}) async-start(), calls=%async_computation.2 | async-start | bytes 5971968 | tf_op jit(solution)/shard_map/reduce_scatter | solution.py:74
  163.9 59.2 %copy-start.3 = (f32[384]{0:T(512)}, f32[384]{0:T(512)S(1)}, u32[]{:S(2)}) copy-start(f32[384]{0:T(512)S(1)} %add_divide_fusion) | copy-start | bytes 4612
  228.9 85.0 %reduce-scatter.7.cloned.1.call-start = ((), (), s32[]{:S(2)}) async-start(), calls=%async_computation.3 | async-start | bytes 1105920
Sparse Core Ops, SparseCore 0:
  229.1 54.9 reduce-scatter.4
  289.3 24.5 reduce-scatter.6
